TPU v7x, 256 devices: a whole 4x4x8 slice. The times are simulated.
256 devices in a mesh: segment: 4 (over y), frame: 16 (over z, core), row: 4 (over x).
Axes of the slice: x: 4, y: 4, z: 8, core: 2. Of those that a mesh axis runs over, the one named last changes fastest.
Arguments:
- latents: bfloat16 [2, 32, 8, 24, 320], P(None, 'frame', 'row')
- cotangent: bfloat16 [2, 32, 8, 24, 320], P(None, 'frame', 'row'), may hold values from -0.0546875 to 0.0546875
- timesteps: int32 [2], replicated, may hold values from 0 to 999
- frame_counts: int32 [2], replicated, may hold values from 8 to 32, as said below
- spatial_weight: bfloat16 [4, 9, 320, 320], P('segment'), may hold values from -0.109375 to 0.109375
- temporal_weight: bfloat16 [4, 3, 320, 320], P('segment'), may hold values from -0.1875 to 0.1875
- time_weight: bfloat16 [4, 1280, 320], P('segment'), may hold values from -0.15625 to 0.15625
- norm_gain: float32 [4, 320], P('segment'), may hold values from 0.5 to 1.5
Outputs:
- spatial_grad: float32 [4, 2880, 320], P('segment', ('frame', 'row'))
- temporal_grad: float32 [4, 960, 320], P('segment', ('frame', 'row'))
- time_grad: float32 [4, 1280, 320], P('segment', ('frame', 'row'))
- gain_grad: float32 [4, 320], P('segment', ('frame', 'row'))
Inputs may be any that keep to these rules, and one draw needn't show every extreme that they name: Frames frame_counts[c] and later of clip c are padding; some clip has all 32 frames.
All inputs are finite; a program needn't handle non-finite values.
Results may differ from a plain program's by a relative error of at most 0.02.
Values may be sent and summed in bfloat16 or wider, within the bound.
No kernel may reach another device: no remote copies, remote signals or barrier semaphores. Data moves between devices by JAX's collectives and lax.ppermute only.
A program may use at most 128 MiB of HBM per device.

v0:
```python
import jax
import jax.numpy as jnp
from jax import lax
from jax.sharding import PartitionSpec as P

C = 320
G = 32
TE = 1280
WIDTH = 24
R_DEV = 2
F_DEV = 2
CLIPS = 2
EPSILON = 1e-05


def with_halo(array, sides, width):
    for axis, dim in sides:
        peers, length = (lax.axis_size(axis), array.shape[dim])
        up = [(i, (i + 1) % peers) for i in range(peers - 1)]
        down = [(j, i) for i, j in up]
        last = lax.slice_in_dim(array, length - width, length, axis=dim)
        leading = lax.slice_in_dim(array, 0, width, axis=dim)
        before = lax.ppermute(last, axis, up)
        after = lax.ppermute(leading, axis, down)
        array = jnp.concatenate([before, array, after], axis=dim)
    return array


def shifted(array, axis, by):
    peers = lax.axis_size(axis)
    pairs = [(i, i + by) for i in range(peers) if 0 <= i + by < peers]
    return lax.ppermute(array, axis, pairs)


def time_features(timesteps):
    half_dim = TE // 2
    frequency = jnp.exp(-jnp.log(10000.0) * jnp.arange(half_dim).astype(jnp.float32) / half_dim)
    angles = timesteps.astype(jnp.float32)[:, None] * frequency[None, :]
    wave_parts = jnp.concatenate([jnp.cos(angles), jnp.sin(angles)], axis=1)
    return jax.nn.silu(wave_parts).astype(jnp.bfloat16)


def group_sum(values):
    per_channel = jnp.sum(values, axis=(0, 1, 2))
    return per_channel.reshape(G, -1).sum(axis=1)


def spread(values):
    return jnp.repeat(values, C // G)


def spatial_columns(padded, row_count, col_count):
    return jnp.concatenate(
        [
            padded[:, vertical : vertical + row_count, lateral : lateral + col_count, :]
            for vertical in range(3)
            for lateral in range(3)
        ],
        axis=-1,
    )


def flip_columns(padded, row_count, col_count):
    return jnp.concatenate(
        [
            padded[
                :, 2 - vertical : 2 - vertical + row_count, 2 - lateral : 2 - lateral + col_count, :
            ]
            for vertical in range(3)
            for lateral in range(3)
        ],
        axis=-1,
    )


def time_columns(padded, frame_count):
    return jnp.concatenate([padded[offset : offset + frame_count] for offset in range(3)], axis=-1)


def time_flip(padded, frame_count):
    return jnp.concatenate(
        [padded[2 - offset : 2 - offset + frame_count] for offset in range(3)], axis=-1
    )


def flat_dot(columns, matrix):
    return jnp.dot(columns.reshape(-1, matrix.shape[0]), matrix, preferred_element_type=jnp.float32)


def outer_dot(columns, right_side):
    return lax.dot_general(
        columns.reshape(-1, columns.shape[-1]),
        right_side.reshape(-1, right_side.shape[-1]),
        (((0,), (0,)), ((), ())),
        preferred_element_type=jnp.float32,
    )


def remember(store, value, clip_index, is_live):
    old_value = lax.dynamic_index_in_dim(store, clip_index, 0, keepdims=False)
    return lax.dynamic_update_index_in_dim(
        store, jnp.where(is_live, value, old_value), clip_index, 0
    )


def pick_row(table, clip_index):
    return lax.dynamic_index_in_dim(table, clip_index, 0, keepdims=False)


def per_device(
    latents,
    cotangent,
    timesteps,
    frame_counts,
    spatial_weight,
    temporal_weight,
    time_weight,
    norm_gain,
):
    sections = lax.axis_size("segment")
    segment_index = lax.axis_index("segment")
    all_rows = R_DEV * lax.axis_size("row")
    group_width = C // G
    tick_total = CLIPS + sections - 1
    act_shape = (F_DEV, R_DEV, WIDTH, C)
    kernel = spatial_weight[0]
    tkernel = temporal_weight[0]
    gain_row = norm_gain[0]
    kernel_flat = kernel.reshape(9 * C, C)
    kernel_back = jnp.transpose(kernel, (0, 2, 1)).reshape(9 * C, C)
    tkernel_flat = tkernel.reshape(3 * C, C)
    tkernel_back = jnp.transpose(tkernel, (0, 2, 1)).reshape(3 * C, C)
    time_embed = time_features(timesteps)
    clip_biases = jnp.dot(time_embed, time_weight[0], preferred_element_type=jnp.float32)
    frame_ids = lax.axis_index("frame") * F_DEV + jnp.arange(F_DEV)
    zero_act = jnp.zeros(act_shape, jnp.bfloat16)

    def frame_mask_of(clip_index):
        frame_limit = pick_row(frame_counts, clip_index)
        frame_mask = (frame_ids < frame_limit).astype(jnp.float32)[:, None, None, None]
        cell_total = frame_limit.astype(jnp.float32) * all_rows * WIDTH * group_width
        return (frame_mask, cell_total)

    padded_in_store = jnp.zeros((CLIPS, F_DEV, R_DEV + 2, WIDTH + 2, C), jnp.bfloat16)
    hidden_store = jnp.zeros((CLIPS,) + act_shape, jnp.float32)
    padded_act_store = jnp.zeros((CLIPS, F_DEV + 2, R_DEV, WIDTH, C), jnp.bfloat16)
    mean_store = jnp.zeros((CLIPS, G), jnp.float32)
    inverse_store = jnp.zeros((CLIPS, G), jnp.float32)
    received = zero_act
    skip_queue = []
    for tick_step in range(tick_total):
        clip_raw = tick_step - segment_index
        is_live = (clip_raw >= 0) & (clip_raw < CLIPS)
        clip_index = jnp.clip(clip_raw, 0, CLIPS - 1)
        first_input = latents[min(tick_step, CLIPS - 1)]
        current = jnp.where(segment_index == 0, first_input, received)
        arriving = skip_queue[tick_step - sections + 1] if tick_step >= sections - 1 else zero_act
        joined = (current.astype(jnp.float32) + arriving.astype(jnp.float32)).astype(jnp.bfloat16)
        current = jnp.where(segment_index == sections - 1, joined, current)
        frame_mask, cell_total = frame_mask_of(clip_index)
        padded_rows = with_halo(current, (("row", 1),), 1)
        padded_in = jnp.pad(padded_rows, ((0, 0), (0, 0), (1, 1), (0, 0)))
        hidden = flat_dot(spatial_columns(padded_in, R_DEV, WIDTH), kernel_flat).reshape(
            act_shape
        ) + pick_row(clip_biases, clip_index)
        masked = hidden * frame_mask
        group_mean = lax.psum(group_sum(masked), ("frame", "row")) / cell_total
        centred = hidden - spread(group_mean)
        variance = (
            lax.psum(group_sum(frame_mask * centred * centred), ("frame", "row")) / cell_total
        )
        inv_spread = lax.rsqrt(variance + EPSILON)
        normed = centred * spread(inv_spread)
        activated = (frame_mask * jax.nn.silu(normed * gain_row)).astype(jnp.bfloat16)
        padded_act = with_halo(activated, (("frame", 0),), 1)
        temporal = flat_dot(time_columns(padded_act, F_DEV), tkernel_flat).reshape(act_shape)
        output = (current.astype(jnp.float32) + temporal).astype(jnp.bfloat16)
        padded_in_store = remember(padded_in_store, padded_in, clip_index, is_live)
        hidden_store = remember(hidden_store, hidden, clip_index, is_live)
        padded_act_store = remember(padded_act_store, padded_act, clip_index, is_live)
        mean_store = remember(mean_store, group_mean, clip_index, is_live)
        inverse_store = remember(inverse_store, inv_spread, clip_index, is_live)
        received = shifted(output, "segment", 1)
        skip_queue.append(shifted(output, "segment", sections - 1))
    spatial_acc = jnp.zeros((9 * C, C), jnp.float32)
    temporal_acc = jnp.zeros((3 * C, C), jnp.float32)
    gain_acc = jnp.zeros((C,), jnp.float32)
    time_acc = jnp.zeros((TE, C), jnp.float32)
    upstream_recv = zero_act
    grad_queue = []
    for tick_step in range(tick_total):
        clip_raw = tick_step - (sections - 1 - segment_index)
        is_live = (clip_raw >= 0) & (clip_raw < CLIPS)
        clip_index = jnp.clip(clip_raw, 0, CLIPS - 1)
        frame_mask, cell_total = frame_mask_of(clip_index)
        last_grad = (frame_mask * pick_row(cotangent, clip_index).astype(jnp.float32)).astype(
            jnp.bfloat16
        )
        upstream = jnp.where(segment_index == sections - 1, last_grad, upstream_recv)
        arriving = grad_queue[tick_step - sections + 1] if tick_step >= sections - 1 else zero_act
        joined = (upstream.astype(jnp.float32) + arriving.astype(jnp.float32)).astype(jnp.bfloat16)
        upstream = jnp.where(segment_index == 0, joined, upstream)
        padded_in = pick_row(padded_in_store, clip_index)
        hidden = pick_row(hidden_store, clip_index)
        padded_act = pick_row(padded_act_store, clip_index)
        group_mean = pick_row(mean_store, clip_index)
        inv_spread = pick_row(inverse_store, clip_index)
        padded_up = with_halo(upstream, (("frame", 0),), 1)
        act_grad = flat_dot(time_flip(padded_up, F_DEV), tkernel_back).reshape(act_shape)
        temporal_part = outer_dot(time_columns(padded_act, F_DEV), upstream)
        normed = (hidden - spread(group_mean)) * spread(inv_spread)
        scaled = normed * gain_row
        gate_sig = jax.nn.sigmoid(scaled)
        scaled_grad = act_grad * frame_mask * gate_sig * (1.0 + scaled * (1.0 - gate_sig))
        gain_part = jnp.sum(scaled_grad * normed, axis=(0, 1, 2))
        normed_grad = scaled_grad * gain_row
        first_total, second_total = lax.psum(
            (group_sum(normed_grad), group_sum(normed_grad * normed)), ("frame", "row")
        )
        first_moment = first_total / cell_total
        second_moment = second_total / cell_total
        hidden_grad = (
            spread(inv_spread)
            * (normed_grad - frame_mask * (spread(first_moment) + normed * spread(second_moment)))
        ).astype(jnp.bfloat16)
        column_sums = jnp.sum(hidden_grad.astype(jnp.float32), axis=(0, 1, 2))
        spatial_part = outer_dot(spatial_columns(padded_in, R_DEV, WIDTH), hidden_grad)
        padded_grad = with_halo(hidden_grad, (("row", 1),), 1)
        padded_grad = jnp.pad(padded_grad, ((0, 0), (0, 0), (1, 1), (0, 0)))
        conv_back = flat_dot(flip_columns(padded_grad, R_DEV, WIDTH), kernel_back).reshape(
            act_shape
        )
        input_grad = (upstream.astype(jnp.float32) + conv_back).astype(jnp.bfloat16)
        spatial_acc = spatial_acc + jnp.where(is_live, spatial_part, 0.0)
        temporal_acc = temporal_acc + jnp.where(is_live, temporal_part, 0.0)
        gain_acc = gain_acc + jnp.where(is_live, gain_part, 0.0)
        embed_row = pick_row(time_embed, clip_index).astype(jnp.float32)
        time_acc = time_acc + jnp.where(is_live, embed_row[:, None] * column_sums[None, :], 0.0)
        upstream_recv = shifted(input_grad, "segment", -1)
        grad_queue.append(shifted(input_grad, "segment", -(sections - 1)))
    spatial_out, temporal_out, time_out, gain_out = (
        lax.psum_scatter(spatial_acc, ("frame", "row"), scatter_dimension=0, tiled=True),
        lax.psum_scatter(temporal_acc, ("frame", "row"), scatter_dimension=0, tiled=True),
        lax.psum_scatter(time_acc, ("frame", "row"), scatter_dimension=0, tiled=True),
        lax.psum_scatter(gain_acc, ("frame", "row"), scatter_dimension=0, tiled=True),
    )
    return (spatial_out[None], temporal_out[None], time_out[None], gain_out[None])


def solution(mesh):
    return jax.shard_map(
        per_device,
        mesh=mesh,
        in_specs=(
            P(None, "frame", "row", None, None),
            P(None, "frame", "row", None, None),
            P(),
            P(),
            P("segment", None, None, None),
            P("segment", None, None, None),
            P("segment", None, None),
            P("segment", None),
        ),
        out_specs=(
            P("segment", ("frame", "row"), None),
            P("segment", ("frame", "row"), None),
            P("segment", ("frame", "row"), None),
            P("segment", ("frame", "row")),
        ),
        check_vma=False,
    )
```

profile of v0, /device:TPU:80, one launch (start us, length us, event | category | flops | bytes accessed | tf_op | source)
XLA Modules:
  0.0 2447.7 jit_solution(5756739828602763937)
XLA Ops:
  53.3 106.2 %psum.140 = f32[32]{0:T(128)S(1)} all-reduce(f32[32]{0:T(128)S(1)} %reduce_sum.451), channel_id=1, replica_groups=mesh['segment'=4,'frame'=16,'row'=4] {'frame','row'}, use_global_device_ids=true, to_apply=%region_2.3 | all-reduce | flops 32 | bytes 256 | tf_op jit(solution)/shard_map/psum | solution.py:167
  160.5 124.5 %psum.141 = f32[32]{0:T(128)S(1)} all-reduce(f32[32]{0:T(128)S(1)} %reduce_sum.453), channel_id=1, replica_groups=mesh['segment'=4,'frame'=16,'row'=4] {'frame','row'}, use_global_device_ids=true, to_apply=%region_5.6 | all-reduce | flops 32 | bytes 256 | tf_op jit(solution)/shard_map/psum | solution.py:170
  286.7 7.3 collective-permute-start.3
  312.5 4.8 collective-permute-start.5
  324.2 118.3 %psum.142 = f32[32]{0:T(128)S(1)} all-reduce(f32[32]{0:T(128)S(1)} %reduce_sum.455), channel_id=1, replica_groups=mesh['segment'=4,'frame'=16,'row'=4] {'frame','row'}, use_global_device_ids=true, to_apply=%region_8.9 | all-reduce | flops 32 | bytes 256 | tf_op jit(solution)/shard_map/psum | solution.py:167
  443.5 125.7 %psum.143 = f32[32]{0:T(128)S(1)} all-reduce(f32[32]{0:T(128)S(1)} %reduce_sum.457), channel_id=1, replica_groups=mesh['segment'=4,'frame'=16,'row'=4] {'frame','row'}, use_global_device_ids=true, to_apply=%region_11.12 | all-reduce | flops 32 | bytes 256 | tf_op jit(solution)/shard_map/psum | solution.py:170
  571.3 5.4 collective-permute-start.8
  606.5 119.5 %psum.144 = f32[32]{0:T(128)S(1)} all-reduce(f32[32]{0:T(128)S(1)} %reduce_sum.459), channel_id=1, replica_groups=mesh['segment'=4,'frame'=16,'row'=4] {'frame','row'}, use_global_device_ids=true, to_apply=%region_14.15 | all-reduce | flops 32 | bytes 256 | tf_op jit(solution)/shard_map/psum | solution.py:167
  727.0 125.7 %psum.145 = f32[32]{0:T(128)S(1)} all-reduce(f32[32]{0:T(128)S(1)} %reduce_sum.461), channel_id=1, replica_groups=mesh['segment'=4,'frame'=16,'row'=4] {'frame','row'}, use_global_device_ids=true, to_apply=%region_17.18 | all-reduce | flops 32 | bytes 256 | tf_op jit(solution)/shard_map/psum | solution.py:170
  854.0 5.6 collective-permute-start.13
  891.2 119.9 %psum.146 = f32[32]{0:T(128)S(1)} all-reduce(f32[32]{0:T(128)S(1)} %reduce_sum.463), channel_id=1, replica_groups=mesh['segment'=4,'frame'=16,'row'=4] {'frame','row'}, use_global_device_ids=true, to_apply=%region_20.21 | all-reduce | flops 32 | bytes 256 | tf_op jit(solution)/shard_map/psum | solution.py:167
  1015.3 125.6 %psum.147 = f32[32]{0:T(128)S(1)} all-reduce(f32[32]{0:T(128)} %reduce_sum.465), channel_id=1, replica_groups=mesh['segment'=4,'frame'=16,'row'=4] {'frame','row'}, use_global_device_ids=true, to_apply=%region_23.24 | all-reduce | flops 32 | bytes 256 | tf_op jit(solution)/shard_map/psum | solution.py:170
  1143.2 5.3 collective-permute-start.19
  1168.1 4.8 collective-permute-start.22
  1180.6 119.4 %psum.148 = f32[32]{0:T(128)S(1)} all-reduce(f32[32]{0:T(128)S(1)} %reduce_sum.467), channel_id=1, replica_groups=mesh['segment'=4,'frame'=16,'row'=4] {'frame','row'}, use_global_device_ids=true, to_apply=%region_26.27 | all-reduce | flops 32 | bytes 256 | tf_op jit(solution)/shard_map/psum | solution.py:167
  1301.4 125.7 %psum.149 = f32[32]{0:T(128)S(1)} all-reduce(f32[32]{0:T(128)S(1)} %reduce_sum.469), channel_id=1, replica_groups=mesh['segment'=4,'frame'=16,'row'=4] {'frame','row'}, use_global_device_ids=true, to_apply=%region_29.30 | all-reduce | flops 32 | bytes 256 | tf_op jit(solution)/shard_map/psum | solution.py:170
  1432.8 124.9 %all-reduce.19 = (f32[32]{0:T(128)S(1)}, f32[32]{0:T(128)S(1)}) all-reduce(f32[32]{0:T(128)S(1)} %reduce_sum.473, f32[32]{0:T(128)S(1)} %reduce_sum.471), channel_id=1, replica_groups=mesh['segment'=4,'frame'=16,'row'=4] {'frame','row'}, use_global_device_ids=true, to_apply=%region_35.36 | all-reduce | flops 64 | bytes 512 | tf_op jit(solution)/shard_map/psum | solution.py:217
  1587.3 9.5 collective-permute-done.29
  1599.9 118.5 %all-reduce.18 = (f32[32]{0:T(128)S(1)}, f32[32]{0:T(128)S(1)}) all-reduce(f32[32]{0:T(128)S(1)} %reduce_sum.477, f32[32]{0:T(128)S(1)} %reduce_sum.475), channel_id=1, replica_groups=mesh['segment'=4,'frame'=16,'row'=4] {'frame','row'}, use_global_device_ids=true, to_apply=%region_41.42 | all-reduce | flops 64 | bytes 512 | tf_op jit(solution)/shard_map/psum | solution.py:217
  1748.5 10.0 collective-permute-done.34
  1761.7 118.0 %all-reduce.17 = (f32[32]{0:T(128)S(1)}, f32[32]{0:T(128)S(1)}) all-reduce(f32[32]{0:T(128)S(1)} %reduce_sum.481, f32[32]{0:T(128)S(1)} %reduce_sum.479), channel_id=1, replica_groups=mesh['segment'=4,'frame'=16,'row'=4] {'frame','row'}, use_global_device_ids=true, to_apply=%region_47.48 | all-reduce | flops 64 | bytes 512 | tf_op jit(solution)/shard_map/psum | solution.py:217
  1927.7 125.8 %all-reduce.16 = (f32[32]{0:T(128)S(1)}, f32[32]{0:T(128)S(1)}) all-reduce(f32[32]{0:T(128)S(1)} %reduce_sum.485, f32[32]{0:T(128)S(1)} %reduce_sum.483), channel_id=1, replica_groups=mesh['segment'=4,'frame'=16,'row'=4] {'frame','row'}, use_global_device_ids=true, to_apply=%region_53.54 | all-reduce | flops 64 | bytes 512 | tf_op jit(solution)/shard_map/psum | solution.py:217
  2087.0 7.7 collective-permute-done.46
  2095.6 117.5 %all-reduce.15 = (f32[32]{0:T(128)S(1)}, f32[32]{0:T(128)S(1)}, f32[320]{0:T(512)S(1)}) all-reduce(f32[32]{0:T(128)S(1)} %reduce_sum.489, f32[32]{0:T(128)S(1)} %reduce_sum.487, f32[320]{0:T(512)S(1)} %select_add_fusion.2), channel_id=1, replica_groups=mesh['segment'=4,'frame'=16,'row'=4] {'frame','row'}, use_global_device_ids=true, to_apply=%region_59.60 | all-reduce | flops 384 | bytes 3072 | tf_op jit(solution)/shard_map/psum | solution.py:217
  2215.6 6.3 collective-permute-start.48
  2226.9 7.5 select_add_fusion
  2237.6 153.2 %fusion.209 = (f32[48,320]{1,0:T(8,128)S(1)}, f32[16,320]{1,0:T(8,128)S(1)}) fusion(f32[2880,320]{1,0:T(8,128)} %select_add_fusion, f32[960,320]{1,0:T(8,128)S(1)} %fusion.2), kind=kCustom, calls=%all-reduce-scatter.2 | all-reduce-scatter fusion | flops 1310722 | bytes 4998144
  2390.8 5.3 collective-permute-start.56
  2396.1 5.4 collective-permute-start.55
  2405.0 8.1 collective-permute-start.57
  2413.7 7.1 collective-permute-start.52
  2425.5 6.8 collective-permute-start.50
  (616 shorter events, 347.0 us)
Async XLA Ops:
  7.2 2432.2 %all-reduce.23.cloned.1.call-start = ((), (), s32[]{:S(2)}) async-start(), calls=%async_computation | async-start | bytes 3932160
  8.3 42.3 %collective-permute-start.1 = (bf16[2,1,24,320]{3,2,1,0:T(8,128)(2,1)S(1)}, bf16[2,1,24,320]{3,2,1,0:T(8,128)(2,1)S(1)}, u32[]{:S(2)}, u32[]{:S(2)}) collective-permute-start(bf16[2,1,24,320]{3,2,1,0:T(8,128)(2,1)S(1)} %get-tuple-element.260), channel_id=1, source_target_pairs={{1,0},{2,1},{3,2},{5,4},{6,5},{7,6},{9,8},{10,9},{11,10},{13,12},{... | collective-permute-start | bytes 92168 | tf_op jit(solution)/shard_map/ppermute | solution.py:24
  9.6 41.0 %collective-permute-start = (bf16[2,1,24,320]{3,2,1,0:T(8,128)(2,1)S(1)}, bf16[2,1,24,320]{3,2,1,0:T(8,128)(2,1)S(1)}, u32[]{:S(2)}, u32[]{:S(2)}) collective-permute-start(bf16[2,1,24,320]{3,2,1,0:T(8,128)(2,1)S(1)} %get-tuple-element.259), channel_id=1, source_target_pairs={{0,1},{1,2},{2,3},{4,5},{5,6},{6,7},{8,9},{9,10},{10,11},{12,13},{... | collective-permute-start | bytes 92168 | tf_op jit(solution)/shard_map/ppermute | solution.py:23
  18.3 1411.3 %collective-permute-start.25 = (bf16[1,2,24,320]{3,2,1,0:T(8,128)(2,1)}, bf16[1,2,24,320]{3,2,1,0:T(8,128)(2,1)}, u32[]{:S(2)}, u32[]{:S(2)}) collective-permute-start(bf16[1,2,24,320]{3,2,1,0:T(8,128)(2,1)} %get-tuple-element.234), channel_id=1, source_target_pairs={{0,4},{4,8},{8,12},{12,16},{16,20},{20,24},{24,28},{28,32},{32,36}... | collective-permute-start | bytes 92168 | tf_op jit(solution)/shard_map/ppermute | solution.py:23
  20.2 1409.4 %collective-permute-start.24 = (bf16[1,2,24,320]{3,2,1,0:T(8,128)(2,1)}, bf16[1,2,24,320]{3,2,1,0:T(8,128)(2,1)}, u32[]{:S(2)}, u32[]{:S(2)}) collective-permute-start(bf16[1,2,24,320]{3,2,1,0:T(8,128)(2,1)} %get-tuple-element.233), channel_id=1, source_target_pairs={{4,0},{8,4},{12,8},{16,12},{20,16},{24,20},{28,24},{32,28},{36,32}... | collective-permute-start | bytes 92168 | tf_op jit(solution)/shard_map/ppermute | solution.py:24
  286.7 12.3 collective-permute-start.3
  293.9 8.6 collective-permute-start.2
  308.6 565.0 %collective-permute-start.15 = (bf16[2,2,24,320]{3,2,1,0:T(8,128)(2,1)}, bf16[2,2,24,320]{3,2,1,0:T(8,128)(2,1)}, u32[]{:S(2)}, u32[]{:S(2)}) collective-permute-start(bf16[2,2,24,320]{3,2,1,0:T(8,128)(2,1)} %fusion.16), channel_id=1, source_target_pairs={{0,192},{1,193},{2,194},{3,195},{4,196},{5,197},{6,198},{7,199},{8... | collective-permute-start | bytes 184328 | tf_op jit(solution)/shard_map/ppermute | solution.py:32
  571.3 12.2 collective-permute-start.8
  576.7 8.9 collective-permute-start.7
  854.0 11.9 collective-permute-start.13
  865.8 295.9 %collective-permute-start.21 = (bf16[2,2,24,320]{3,2,1,0:T(8,128)(2,1)}, bf16[2,2,24,320]{3,2,1,0:T(8,128)(2,1)}, u32[]{:S(2)}, u32[]{:S(2)}) collective-permute-start(bf16[2,2,24,320]{3,2,1,0:T(8,128)(2,1)} %copy-done.98), channel_id=1, source_target_pairs={{0,192},{1,193},{2,194},{3,195},{4,196},{5,197},{6,198},{7,199},{8... | collective-permute-start | bytes 184328 | tf_op jit(solution)/shard_map/ppermute | solution.py:32
  1143.2 9.1 collective-permute-start.19
  1583.6 13.1 collective-permute-start.29
  1745.2 13.2 collective-permute-start.34
  1888.2 11.8 collective-permute-start.39
  1904.0 21.8 collective-permute-start.41
  1908.7 17.1 collective-permute-start.40
  2054.1 11.3 collective-permute-start.43
  2055.4 10.0 collective-permute-start.42
  2064.1 11.3 collective-permute-start.45
  2077.2 9.8 collective-permute-start.47
  2082.0 12.8 collective-permute-start.46
  2213.7 20.8 collective-permute-start.49
  2215.6 18.9 collective-permute-start.48
  2390.8 34.7 %collective-permute-start.56 = (f32[16,320]{1,0:T(8,128)S(1)}, f32[16,320]{1,0:T(8,128)S(1)}, u32[]{:S(2)}, u32[]{:S(2)}) collective-permute-start(f32[16,320]{1,0:T(8,128)S(1)} %get-tuple-element.55), channel_id=1, source_target_pairs={{0,3},{1,4},{2,5},{3,6},{4,7},{5,8},{6,9},{7,10},{8,11},{9,12},{10... | collective-permute-start | bytes 61448
  2396.1 36.2 %collective-permute-start.55 = (f32[16,320]{1,0:T(8,128)S(1)}, f32[16,320]{1,0:T(8,128)S(1)}, u32[]{:S(2)}, u32[]{:S(2)}) collective-permute-start(f32[16,320]{1,0:T(8,128)S(1)} %get-tuple-element.55), channel_id=1, source_target_pairs={{0,2},{1,3},{2,4},{3,5},{4,6},{5,7},{6,8},{7,9},{8,10},{9,11},{10,... | collective-permute-start | bytes 61448
  2401.5 32.8 %collective-permute-start.54 = (f32[16,320]{1,0:T(8,128)S(1)}, f32[16,320]{1,0:T(8,128)S(1)}, u32[]{:S(2)}, u32[]{:S(2)}) collective-permute-start(f32[16,320]{1,0:T(8,128)S(1)} %get-tuple-element.55), channel_id=1, source_target_pairs={{0,1},{1,2},{2,3},{3,4},{4,5},{5,6},{6,7},{7,8},{8,9},{9,10},{10,1... | collective-permute-start | bytes 61448
  2405.0 15.8 collective-permute-start.57
  2413.7 24.3 collective-permute-start.52
  2420.8 17.2 collective-permute-start.51
  2425.5 12.5 collective-permute-start.50
  (126 other events, 4954.7 us)
Sparse Core Ops, SparseCore 0:
  2224.7 204.9 all-reduce.22
where the time goes:
time: 2450 us
  blocking collectives  1970 us (80%)
  starting transfers between devices  203 us (8%)
  local copies, waits for them, and re-layouts  80.7 us (3%)
  waiting for transfers between devices  61.5 us (3%)
  other arithmetic  55.7 us (2%)
  matrix products  53.3 us (2%)
  between operations  25.5 us (1%)
    psum x5, blocking collectives, per_device(): lax.psum(group_sum(frame_mask * centred * centred), ('frame', 'row'))  627 us
    psum x5, blocking collectives, per_device(): lax.psum((group_sum(normed_grad), group_sum(normed_grad * normed)), ('fra...  605 us
    psum x5, blocking collectives, per_device(): group_mean = lax.psum(group_sum(masked), ('frame', 'row')) / cell_total  583 us
    unnamed x1, blocking collectives  153 us
    ppermute x19, starting transfers between devices, with_halo(): before = lax.ppermute(last, axis, up)  78.6 us
  transfers between devices with their start and end apart: 59, of which 22 were waited for; matrix products, arithmetic and copies ran while one was open for 12% of the time, Pallas kernels for 0%

commit v1 on v0

--- a/solution.py
+++ b/solution.py
@@ -164,7 +164,7 @@
             act_shape
         ) + pick_row(clip_biases, clip_index)
         masked = hidden * frame_mask
-        group_mean = lax.psum(group_sum(masked), ("frame", "row")) / cell_total
+        group_mean = lax.psum(lax.psum(group_sum(masked), "frame"), "row") / cell_total
         centred = hidden - spread(group_mean)
         variance = (
             lax.psum(group_sum(frame_mask * centred * centred), ("frame", "row")) / cell_total

time: 2450 us -> 1990 us (0.81)
  blocking collectives: 1970 us -> 1500 us
    psum x5 -> x10, blocking collectives: 583 us -> 206 us  [the longest x5 156 us: per_device(): lax.psum(group_sum(masked), 'frame')]
    psum x5, blocking collectives: 627 us -> 533 us  [per_device(): lax.psum(group_sum(frame_mask * centred * centred), ('frame', 'row'))]
  transfers between devices with their start and end apart: 59 -> 59, of which waited for: 22 -> 22; matrix products, arithmetic and copies ran while one was open for 12% -> 15% of each run, Pallas kernels for 0% -> 0%
where the time goes in v1:
time: 1990 us
  blocking collectives  1500 us (75%)
  starting transfers between devices  207 us (10%)
  local copies, waits for them, and re-layouts  80.3 us (4%)
  waiting for transfers between devices  65.1 us (3%)
  other arithmetic  55.2 us (3%)
  matrix products  53.2 us (3%)
  between operations  25.3 us (1%)
    psum x5, blocking collectives, per_device(): lax.psum((group_sum(normed_grad), group_sum(normed_grad * normed)), ('fra...  605 us
    psum x5, blocking collectives, per_device(): lax.psum(group_sum(frame_mask * centred * centred), ('frame', 'row'))  533 us
    psum x5, blocking collectives, per_device(): lax.psum(group_sum(masked), 'frame')  156 us
    unnamed x1, blocking collectives  155 us
    ppermute x19, starting transfers between devices, with_halo(): before = lax.ppermute(last, axis, up)  74.9 us
    ppermute x19, starting transfers between devices, with_halo(): after = lax.ppermute(leading, axis, down)  58.3 us
    psum x5, blocking collectives, per_device(): lax.psum(lax.psum(group_sum(masked), 'frame'), 'row') / cell_total  50 us
    unnamed x9, starting transfers between devices  41.2 us
  transfers between devices with their start and end apart: 59, of which 22 were waited for; matrix products, arithmetic and copies ran while one was open for 15% of the time, Pallas kernels for 0%

profile of v1, /device:TPU:80, one launch (start us, length us, event | category | flops | bytes accessed | tf_op | source)
XLA Modules:
  0.0 1985.7 jit_solution(13956408605843367700)
XLA Ops:
  52.9 22.4 %psum.175 = f32[32]{0:T(128)S(1)} all-reduce(f32[32]{0:T(128)S(1)} %reduce_sum.451), channel_id=1, replica_groups=mesh['segment'=4,'frame'=16,'row'=4] {'frame'}, use_global_device_ids=true, to_apply=%region_2.3 | all-reduce | flops 32 | bytes 256 | tf_op jit(solution)/shard_map/psum | solution.py:167
  75.3 9.2 psum.176
  85.5 106.5 %psum.177 = f32[32]{0:T(128)S(1)} all-reduce(f32[32]{0:T(128)S(1)} %reduce_sum.453), channel_id=1, replica_groups=mesh['segment'=4,'frame'=16,'row'=4] {'frame','row'}, use_global_device_ids=true, to_apply=%region_6.7 | all-reduce | flops 32 | bytes 256 | tf_op jit(solution)/shard_map/psum | solution.py:170
  193.6 9.0 collective-permute-start.3
  232.8 32.6 %psum.178 = f32[32]{0:T(128)S(1)} all-reduce(f32[32]{0:T(128)S(1)} %reduce_sum.455), channel_id=1, replica_groups=mesh['segment'=4,'frame'=16,'row'=4] {'frame'}, use_global_device_ids=true, to_apply=%region_9.10 | all-reduce | flops 32 | bytes 256 | tf_op jit(solution)/shard_map/psum | solution.py:167
  265.4 10.1 psum.179
  276.5 106.5 %psum.180 = f32[32]{0:T(128)S(1)} all-reduce(f32[32]{0:T(128)S(1)} %reduce_sum.457), channel_id=1, replica_groups=mesh['segment'=4,'frame'=16,'row'=4] {'frame','row'}, use_global_device_ids=true, to_apply=%region_13.14 | all-reduce | flops 32 | bytes 256 | tf_op jit(solution)/shard_map/psum | solution.py:170
  385.2 7.9 collective-permute-start.8
  422.5 33.9 %psum.181 = f32[32]{0:T(128)S(1)} all-reduce(f32[32]{0:T(128)S(1)} %reduce_sum.459), channel_id=1, replica_groups=mesh['segment'=4,'frame'=16,'row'=4] {'frame'}, use_global_device_ids=true, to_apply=%region_16.17 | all-reduce | flops 32 | bytes 256 | tf_op jit(solution)/shard_map/psum | solution.py:167
  456.3 10.1 psum.182
  467.5 106.6 %psum.183 = f32[32]{0:T(128)S(1)} all-reduce(f32[32]{0:T(128)S(1)} %reduce_sum.461), channel_id=1, replica_groups=mesh['segment'=4,'frame'=16,'row'=4] {'frame','row'}, use_global_device_ids=true, to_apply=%region_20.21 | all-reduce | flops 32 | bytes 256 | tf_op jit(solution)/shard_map/psum | solution.py:170
  575.4 8.2 collective-permute-start.13
  614.9 34.1 %psum.184 = f32[32]{0:T(128)S(1)} all-reduce(f32[32]{0:T(128)S(1)} %reduce_sum.463), channel_id=1, replica_groups=mesh['segment'=4,'frame'=16,'row'=4] {'frame'}, use_global_device_ids=true, to_apply=%region_23.24 | all-reduce | flops 32 | bytes 256 | tf_op jit(solution)/shard_map/psum | solution.py:167
  649.1 10.3 psum.185
  663.4 106.8 %psum.186 = f32[32]{0:T(128)S(1)} all-reduce(f32[32]{0:T(128)} %reduce_sum.465), channel_id=1, replica_groups=mesh['segment'=4,'frame'=16,'row'=4] {'frame','row'}, use_global_device_ids=true, to_apply=%region_27.28 | all-reduce | flops 32 | bytes 256 | tf_op jit(solution)/shard_map/psum | solution.py:170
  772.3 8.0 collective-permute-start.19
  812.7 33.2 %psum.187 = f32[32]{0:T(128)S(1)} all-reduce(f32[32]{0:T(128)S(1)} %reduce_sum.467), channel_id=1, replica_groups=mesh['segment'=4,'frame'=16,'row'=4] {'frame'}, use_global_device_ids=true, to_apply=%region_30.31 | all-reduce | flops 32 | bytes 256 | tf_op jit(solution)/shard_map/psum | solution.py:167
  845.9 10.3 psum.188
  857.6 106.5 %psum.189 = f32[32]{0:T(128)S(1)} all-reduce(f32[32]{0:T(128)S(1)} %reduce_sum.469), channel_id=1, replica_groups=mesh['segment'=4,'frame'=16,'row'=4] {'frame','row'}, use_global_device_ids=true, to_apply=%region_34.35 | all-reduce | flops 32 | bytes 256 | tf_op jit(solution)/shard_map/psum | solution.py:170
  969.9 125.0 %all-reduce.19 = (f32[32]{0:T(128)S(1)}, f32[32]{0:T(128)S(1)}) all-reduce(f32[32]{0:T(128)S(1)} %reduce_sum.473, f32[32]{0:T(128)S(1)} %reduce_sum.471), channel_id=1, replica_groups=mesh['segment'=4,'frame'=16,'row'=4] {'frame','row'}, use_global_device_ids=true, to_apply=%region_40.41 | all-reduce | flops 64 | bytes 512 | tf_op jit(solution)/shard_map/psum | solution.py:217
  1124.4 9.5 collective-permute-done.29
  1137.1 119.3 %all-reduce.18 = (f32[32]{0:T(128)S(1)}, f32[32]{0:T(128)S(1)}) all-reduce(f32[32]{0:T(128)S(1)} %reduce_sum.477, f32[32]{0:T(128)S(1)} %reduce_sum.475), channel_id=1, replica_groups=mesh['segment'=4,'frame'=16,'row'=4] {'frame','row'}, use_global_device_ids=true, to_apply=%region_46.47 | all-reduce | flops 64 | bytes 512 | tf_op jit(solution)/shard_map/psum | solution.py:217
  1286.5 10.0 collective-permute-done.34
  1299.7 118.0 %all-reduce.17 = (f32[32]{0:T(128)S(1)}, f32[32]{0:T(128)S(1)}) all-reduce(f32[32]{0:T(128)S(1)} %reduce_sum.481, f32[32]{0:T(128)S(1)} %reduce_sum.479), channel_id=1, replica_groups=mesh['segment'=4,'frame'=16,'row'=4] {'frame','row'}, use_global_device_ids=true, to_apply=%region_52.53 | all-reduce | flops 64 | bytes 512 | tf_op jit(solution)/shard_map/psum | solution.py:217
  1465.8 125.6 %all-reduce.16 = (f32[32]{0:T(128)S(1)}, f32[32]{0:T(128)S(1)}) all-reduce(f32[32]{0:T(128)S(1)} %reduce_sum.485, f32[32]{0:T(128)S(1)} %reduce_sum.483), channel_id=1, replica_groups=mesh['segment'=4,'frame'=16,'row'=4] {'frame','row'}, use_global_device_ids=true, to_apply=%region_58.59 | all-reduce | flops 64 | bytes 512 | tf_op jit(solution)/shard_map/psum | solution.py:217
  1624.9 7.7 collective-permute-done.46
  1633.5 117.5 %all-reduce.15 = (f32[32]{0:T(128)S(1)}, f32[32]{0:T(128)S(1)}, f32[320]{0:T(512)S(1)}) all-reduce(f32[32]{0:T(128)S(1)} %reduce_sum.489, f32[32]{0:T(128)S(1)} %reduce_sum.487, f32[320]{0:T(512)S(1)} %select_add_fusion.2), channel_id=1, replica_groups=mesh['segment'=4,'frame'=16,'row'=4] {'frame','row'}, use_global_device_ids=true, to_apply=%region_64.65 | all-reduce | flops 384 | bytes 3072 | tf_op jit(solution)/shard_map/psum | solution.py:217
  1764.8 7.5 select_add_fusion
  1775.4 154.9 %fusion.209 = (f32[48,320]{1,0:T(8,128)S(1)}, f32[16,320]{1,0:T(8,128)S(1)}) fusion(f32[2880,320]{1,0:T(8,128)} %select_add_fusion, f32[960,320]{1,0:T(8,128)S(1)} %fusion.2), kind=kCustom, calls=%all-reduce-scatter.2 | all-reduce-scatter fusion | flops 1310722 | bytes 4998144
  1942.7 8.0 collective-permute-start.57
  1951.3 6.6 collective-permute-start.52
  1963.5 6.8 collective-permute-start.50
  (621 shorter events, 371.8 us)
Async XLA Ops:
  7.2 1970.3 %all-reduce.23.cloned.1.call-start = ((), (), s32[]{:S(2)}) async-start(), calls=%async_computation | async-start | bytes 3932160
  8.3 41.8 %collective-permute-start.1 = (bf16[2,1,24,320]{3,2,1,0:T(8,128)(2,1)S(1)}, bf16[2,1,24,320]{3,2,1,0:T(8,128)(2,1)S(1)}, u32[]{:S(2)}, u32[]{:S(2)}) collective-permute-start(bf16[2,1,24,320]{3,2,1,0:T(8,128)(2,1)S(1)} %get-tuple-element.260), channel_id=1, source_target_pairs={{1,0},{2,1},{3,2},{5,4},{6,5},{7,6},{9,8},{10,9},{11,10},{13,12},{... | collective-permute-start | bytes 92168 | tf_op jit(solution)/shard_map/ppermute | solution.py:24
  9.6 40.5 %collective-permute-start = (bf16[2,1,24,320]{3,2,1,0:T(8,128)(2,1)S(1)}, bf16[2,1,24,320]{3,2,1,0:T(8,128)(2,1)S(1)}, u32[]{:S(2)}, u32[]{:S(2)}) collective-permute-start(bf16[2,1,24,320]{3,2,1,0:T(8,128)(2,1)S(1)} %get-tuple-element.259), channel_id=1, source_target_pairs={{0,1},{1,2},{2,3},{4,5},{5,6},{6,7},{8,9},{9,10},{10,11},{12,13},{... | collective-permute-start | bytes 92168 | tf_op jit(solution)/shard_map/ppermute | solution.py:23
  18.2 948.4 %collective-permute-start.25 = (bf16[1,2,24,320]{3,2,1,0:T(8,128)(2,1)}, bf16[1,2,24,320]{3,2,1,0:T(8,128)(2,1)}, u32[]{:S(2)}, u32[]{:S(2)}) collective-permute-start(bf16[1,2,24,320]{3,2,1,0:T(8,128)(2,1)} %get-tuple-element.234), channel_id=1, source_target_pairs={{0,4},{4,8},{8,12},{12,16},{16,20},{20,24},{24,28},{28,32},{32,36}... | collective-permute-start | bytes 92168 | tf_op jit(solution)/shard_map/ppermute | solution.py:23
  20.1 946.5 %collective-permute-start.24 = (bf16[1,2,24,320]{3,2,1,0:T(8,128)(2,1)}, bf16[1,2,24,320]{3,2,1,0:T(8,128)(2,1)}, u32[]{:S(2)}, u32[]{:S(2)}) collective-permute-start(bf16[1,2,24,320]{3,2,1,0:T(8,128)(2,1)} %get-tuple-element.233), channel_id=1, source_target_pairs={{4,0},{8,4},{12,8},{16,12},{20,16},{24,20},{28,24},{32,28},{36,32}... | collective-permute-start | bytes 92168 | tf_op jit(solution)/shard_map/ppermute | solution.py:24
  193.6 13.9 collective-permute-start.3
  202.6 8.5 collective-permute-start.2
  217.2 380.4 %collective-permute-start.15 = (bf16[2,2,24,320]{3,2,1,0:T(8,128)(2,1)}, bf16[2,2,24,320]{3,2,1,0:T(8,128)(2,1)}, u32[]{:S(2)}, u32[]{:S(2)}) collective-permute-start(bf16[2,2,24,320]{3,2,1,0:T(8,128)(2,1)} %fusion.16), channel_id=1, source_target_pairs={{0,192},{1,193},{2,194},{3,195},{4,196},{5,197},{6,198},{7,199},{8... | collective-permute-start | bytes 184328 | tf_op jit(solution)/shard_map/ppermute | solution.py:32
  385.2 13.9 collective-permute-start.8
  393.1 8.8 collective-permute-start.7
  575.4 13.6 collective-permute-start.13
  589.0 204.6 %collective-permute-start.21 = (bf16[2,2,24,320]{3,2,1,0:T(8,128)(2,1)}, bf16[2,2,24,320]{3,2,1,0:T(8,128)(2,1)}, u32[]{:S(2)}, u32[]{:S(2)}) collective-permute-start(bf16[2,2,24,320]{3,2,1,0:T(8,128)(2,1)} %copy-done.98), channel_id=1, source_target_pairs={{0,192},{1,193},{2,194},{3,195},{4,196},{5,197},{6,198},{7,199},{8... | collective-permute-start | bytes 184328 | tf_op jit(solution)/shard_map/ppermute | solution.py:32
  772.3 10.8 collective-permute-start.19
  1120.8 13.2 collective-permute-start.29
  1283.2 13.2 collective-permute-start.34
  1426.1 11.7 collective-permute-start.39
  1441.9 21.9 %collective-permute-start.41 = (bf16[1,2,24,320]{3,2,1,0:T(8,128)(2,1)}, bf16[1,2,24,320]{3,2,1,0:T(8,128)(2,1)}, u32[]{:S(2)}, u32[]{:S(2)}) collective-permute-start(bf16[1,2,24,320]{3,2,1,0:T(8,128)(2,1)} %get-tuple-element.214), channel_id=1, source_target_pairs={{0,4},{4,8},{8,12},{12,16},{16,20},{20,24},{24,28},{28,32},{32,36}... | collective-permute-start | bytes 92168 | tf_op jit(solution)/shard_map/ppermute | solution.py:23
  1446.6 17.2 collective-permute-start.40
  1592.0 11.3 collective-permute-start.43
  1593.3 10.0 collective-permute-start.42
  1601.9 11.2 collective-permute-start.45
  1615.1 9.8 collective-permute-start.47
  1619.8 12.8 collective-permute-start.46
  1751.5 20.8 %collective-permute-start.49 = (bf16[1,2,24,320]{3,2,1,0:T(8,128)(2,1)S(1)}, bf16[1,2,24,320]{3,2,1,0:T(8,128)(2,1)S(1)}, u32[]{:S(2)}, u32[]{:S(2)}) collective-permute-start(bf16[1,2,24,320]{3,2,1,0:T(8,128)(2,1)S(1)} %get-tuple-element.206), channel_id=1, source_target_pairs={{4,0},{8,4},{12,8},{16,12},{20,16},{24,20},{28,24},{32,28},{36,32}... | collective-permute-start | bytes 92168 | tf_op jit(solution)/shard_map/ppermute | solution.py:24
  1753.5 18.8 collective-permute-start.48
  1930.4 33.1 %collective-permute-start.56 = (f32[16,320]{1,0:T(8,128)S(1)}, f32[16,320]{1,0:T(8,128)S(1)}, u32[]{:S(2)}, u32[]{:S(2)}) collective-permute-start(f32[16,320]{1,0:T(8,128)S(1)} %get-tuple-element.55), channel_id=1, source_target_pairs={{0,3},{1,4},{2,5},{3,6},{4,7},{5,8},{6,9},{7,10},{8,11},{9,12},{10... | collective-permute-start | bytes 61448
  1935.3 35.0 %collective-permute-start.55 = (f32[16,320]{1,0:T(8,128)S(1)}, f32[16,320]{1,0:T(8,128)S(1)}, u32[]{:S(2)}, u32[]{:S(2)}) collective-permute-start(f32[16,320]{1,0:T(8,128)S(1)} %get-tuple-element.55), channel_id=1, source_target_pairs={{0,2},{1,3},{2,4},{3,5},{4,6},{5,7},{6,8},{7,9},{8,10},{9,11},{10,... | collective-permute-start | bytes 61448
  1938.9 33.3 %collective-permute-start.54 = (f32[16,320]{1,0:T(8,128)S(1)}, f32[16,320]{1,0:T(8,128)S(1)}, u32[]{:S(2)}, u32[]{:S(2)}) collective-permute-start(f32[16,320]{1,0:T(8,128)S(1)} %get-tuple-element.55), channel_id=1, source_target_pairs={{0,1},{1,2},{2,3},{3,4},{4,5},{5,6},{6,7},{7,8},{8,9},{9,10},{10,1... | collective-permute-start | bytes 61448
  1942.7 15.2 collective-permute-start.57
  1951.3 24.7 %collective-permute-start.52 = (f32[48,320]{1,0:T(8,128)S(1)}, f32[48,320]{1,0:T(8,128)S(1)}, u32[]{:S(2)}, u32[]{:S(2)}) collective-permute-start(f32[48,320]{1,0:T(8,128)S(1)} %get-tuple-element.54), channel_id=1, source_target_pairs={{0,3},{1,4},{2,5},{3,6},{4,7},{5,8},{6,9},{7,10},{8,11},{9,12},{10... | collective-permute-start | bytes 184328
  1957.9 18.1 collective-permute-start.51
  1963.5 12.5 collective-permute-start.50
  (126 other events, 4342.7 us)
Sparse Core Ops, SparseCore 0:
  1762.5 205.2 all-reduce.22
